TPU v7x, 256 devices: a whole 4x4x8 slice. The times are simulated.
256 devices in a mesh: wide: 32 (over z_hi, x, core), narrow: 8 (over z_lo, y).
Axes of the slice: x: 4, y: 4, z: 8 (z_hi: 4, z_lo: 2; z = z_hi * 2 + z_lo), core: 2. Of those that a mesh axis runs over, the one named last changes fastest.
Arguments:
- three_index: bfloat16 [32, 3072, 1024], P('wide', None, 'narrow'), may hold values from -0.59765625 to 0.59765625
- orbital_map: int32 [32], replicated, may hold values from 0 to 31, each once
- occ_energy: float32 [32], replicated, may hold values from -2 to -0.3
- vir_energy: float32 [1024], replicated, may hold values from 0.2 to 3
- pair_kept: int32 [6, 32], P(None, 'wide'), may hold values 0 or 1
Outputs:
- density: float32 [32, 3072, 1024], P('wide', None, 'narrow')
Inputs may be any that keep to these rules, and one draw needn't show every extreme that they name: `orbital_map`: each of the 32 orbitals once.
All inputs are finite; a program needn't handle non-finite values. No bound on the sum of `pair_kept` on one device may be relied on, other than what follows from the above.
Results may differ from a plain program's by a relative error of at most 0.0015.
Values may be sent and summed in bfloat16 or wider, within the bound.
A program may use at most 192 MiB of HBM per device.

v0:
```python
import jax
import jax.numpy as jnp
from jax import lax
from jax.sharding import PartitionSpec as P

ROUNDS = 5


def passed_along(array, axis, by):
    length = lax.axis_size(axis)
    return lax.ppermute(array, axis, [(i, (i + by) % length) for i in range(length)])


def block_energy(orbital_map, occ_energy, block_id, occ_count):
    orbits = lax.dynamic_slice_in_dim(orbital_map, block_id * occ_count, occ_count)
    labels = jnp.arange(occ_energy.shape[0], dtype=jnp.int32)
    chosen = orbits[:, None] == labels[None, :]
    return jnp.sum(jnp.where(chosen, occ_energy[None, :], 0.0), axis=1)


def amplitudes(gathered, visiting, left_energy, right_energy, vir_all, vir_local, weight):
    coulomb = jnp.einsum("ipa,jpb->ijab", gathered, visiting, preferred_element_type=jnp.float32)
    denominator = (vir_all[:, None] + vir_local[None, :])[None, None] - (
        left_energy[:, None] + right_energy[None, :]
    )[:, :, None, None]
    return (weight * coulomb / denominator).astype(jnp.bfloat16)


def per_device(three_index, orbital_map, occ_energy, vir_energy, pair_kept):
    occ_count = three_index.shape[0]
    vir_count = three_index.shape[2]
    blocks = lax.axis_size("wide")
    own_block = lax.axis_index("wide")
    vir_local = lax.dynamic_slice_in_dim(
        vir_energy, lax.axis_index("narrow") * vir_count, vir_count
    )
    own_energy = block_energy(orbital_map, occ_energy, own_block, occ_count)
    weights = pair_kept.astype(jnp.float32)
    gathered = lax.all_gather(three_index, "narrow", axis=2, tiled=True)
    amplitude = amplitudes(
        gathered, three_index, own_energy, own_energy, vir_energy, vir_local, weights[0, 0]
    )
    forward = jnp.einsum(
        "ijab,jpb->ipa", amplitude, three_index, preferred_element_type=jnp.float32
    )
    visiting = three_index
    stored_amps = []
    for round_index in range(1, ROUNDS + 1):
        visiting = passed_along(visiting, "wide", 1)
        partner = (own_block - round_index) % blocks
        partner_energy = block_energy(orbital_map, occ_energy, partner, occ_count)
        amplitude = amplitudes(
            gathered,
            visiting,
            own_energy,
            partner_energy,
            vir_energy,
            vir_local,
            weights[round_index, 0],
        )
        forward = forward + jnp.einsum(
            "ijab,jpb->ipa", amplitude, visiting, preferred_element_type=jnp.float32
        )
        stored_amps.append(amplitude)
    carried = None
    for round_index in range(1, ROUNDS + 1):
        backward = jnp.einsum(
            "ijab,ipa->jpb",
            stored_amps[round_index - 1],
            gathered,
            preferred_element_type=jnp.float32,
        )
        if round_index > 1:
            carried = passed_along(carried, "wide", 1) + backward
        else:
            carried = backward
    returned = passed_along(carried, "wide", -ROUNDS)
    scattered = lax.psum_scatter(forward, "narrow", scatter_dimension=2, tiled=True)
    return scattered + returned


def solution(mesh):
    placed = (P("wide", None, "narrow"), P(), P(), P(), P(None, "wide"))
    return jax.shard_map(
        per_device, mesh=mesh, in_specs=placed, out_specs=P("wide", None, "narrow"), check_vma=False
    )
```

profile of v0, /device:TPU:64, one launch (start us, length us, event | category | flops | bytes accessed | tf_op | source)
XLA Modules:
  0.0 543.8 jit_solution(8355151380968970125)
XLA Ops:
  6.5 0.0 all-gather.2.cloned.1.call-start
  6.5 0.7 all-gather.2.cloned.1.call-update
  7.3 0.0 reduce-scatter.2.cloned.1.call-start
  7.3 0.1 collective-permute-start
  7.4 17.1 %collective-permute-done = bf16[1,3072,128]{2,1,0:T(8,128)(2,1)S(1)} collective-permute-done((bf16[1,3072,128]{2,1,0:T(8,128)(2,1)}, bf16[1,3072,128]{2,1,0:T(8,128)(2,1)S(1)}, u32[]{:S(2)}, u32[]{:S(2)}) %collective-permute-start) | collective-permute-done | bytes 786464 | tf_op jit(solution)/shard_map/ppermute | solution.py:11
  24.5 0.0 collective-permute-start.1
  24.5 58.5 %collective-permute-done.1 = bf16[1,3072,128]{2,1,0:T(8,128)(2,1)S(1)} collective-permute-done((bf16[1,3072,128]{2,1,0:T(8,128)(2,1)S(1)}, bf16[1,3072,128]{2,1,0:T(8,128)(2,1)S(1)}, u32[]{:S(2)}, u32[]{:S(2)}) %collective-permute-start.1) | collective-permute-done | bytes 786464 | tf_op jit(solution)/shard_map/ppermute | solution.py:11
  83.1 0.0 collective-permute-start.2
  83.1 38.9 %collective-permute-done.2 = bf16[1,3072,128]{2,1,0:T(8,128)(2,1)S(1)} collective-permute-done((bf16[1,3072,128]{2,1,0:T(8,128)(2,1)S(1)}, bf16[1,3072,128]{2,1,0:T(8,128)(2,1)S(1)}, u32[]{:S(2)}, u32[]{:S(2)}) %collective-permute-start.2) | collective-permute-done | bytes 786464 | tf_op jit(solution)/shard_map/ppermute | solution.py:11
  122.0 0.0 collective-permute-start.3
  122.0 1.6 fusion.160
  123.6 5.2 fusion.158
  136.2 0.7 convert_element_type.21
  136.9 0.8 dynamic_slice.21
  137.6 0.7 fusion.159
  138.3 0.0 copy-done.1
  138.3 10.8 %collective-permute-done.3 = bf16[1,3072,128]{2,1,0:T(8,128)(2,1)S(1)} collective-permute-done((bf16[1,3072,128]{2,1,0:T(8,128)(2,1)S(1)}, bf16[1,3072,128]{2,1,0:T(8,128)(2,1)S(1)}, u32[]{:S(2)}, u32[]{:S(2)}) %collective-permute-start.3) | collective-permute-done | bytes 786464 | tf_op jit(solution)/shard_map/ppermute | solution.py:11
  149.1 0.0 collective-permute-start.4
  149.1 0.0 slice-start
  149.1 5.2 fusion.109
  154.3 0.0 copy-done.2
  154.3 0.0 slice-start.1
  154.4 0.0 copy-start.7
  154.4 6.4 %fusion.141 = f32[1024,3072]{1,0:T(8,128)} fusion(bf16[1024,128]{0,1:T(8,128)(2,1)S(1)} %fusion.109, bf16[1,3072,128]{2,1,0:T(8,128)(2,1)S(1)} %copy-done.2), kind=kOutput, calls=%fused_computation.74 | convolution fusion | flops 805306368 | bytes 13631488 | tf_op jit(solution)/shard_map/ijab,jpb->ipa/dot_general | solution.py:61
  160.8 0.0 slice-done
  160.8 0.0 slice-done.1
  160.8 0.0 copy-done.7
  160.8 1.6 fusion.118
  162.4 0.0 copy-start.5
  162.4 6.3 %fusion.144 = f32[1024,3072]{1,0:T(8,128)} fusion(bf16[1024,128]{0,1:T(8,128)(2,1)S(1)} %fusion.118, bf16[1,3072,128]{2,1,0:T(8,128)(2,1)S(1)} %collective-permute-done), kind=kOutput, calls=%fused_computation.77 | convolution fusion | flops 805306368 | bytes 13631488 | tf_op jit(solution)/shard_map/ijab,jpb->ipa/dot_general | solution.py:61
  168.7 0.0 copy-done.5
  168.7 1.7 fusion.100
  170.4 6.4 %fusion.138 = f32[1024,3072]{1,0:T(8,128)} fusion(bf16[1024,128]{0,1:T(8,128)(2,1)S(1)} %fusion.100, bf16[1,3072,128]{2,1,0:T(8,128)(2,1)S(1)} %collective-permute-done.2), kind=kOutput, calls=%fused_computation.71 | convolution fusion | flops 805306368 | bytes 13631488 | tf_op jit(solution)/shard_map/ijab,jpb->ipa/dot_general | solution.py:61
  176.8 0.0 copy-done.3
  176.8 1.7 fusion.91
  178.5 0.0 copy-start
  178.5 6.3 %fusion.135 = f32[1024,3072]{1,0:T(8,128)} fusion(bf16[1024,128]{0,1:T(8,128)(2,1)S(1)} %fusion.91, bf16[1,3072,128]{2,1,0:T(8,128)(2,1)S(1)} %collective-permute-done.3), kind=kOutput, calls=%fused_computation.68 | convolution fusion | flops 805306368 | bytes 13631488 | tf_op jit(solution)/shard_map/ijab,jpb->ipa/dot_general | solution.py:61
  184.8 11.0 %fusion.131 = f32[1024,3072]{1,0:T(8,128)} fusion(bf16[1,3072,1024]{2,1,0:T(8,128)(2,1)} %all-gather.2.cloned.1.call-done, bf16[1,3072,128]{2,1,0:T(8,128)(2,1)S(1)} %copy-done, f32[]{:T(128)S(6)} %add.191, f32[128]{0:T(128)S(1)} %dynamic_slice.21, f32[1024]{0:T(1024)S(1)} %copy-done.7, f32[]{:T(128)} %bitcast), kind=kOutput, calls=%fused_computation.65 | convolution fusion | flops 1611268096 | bytes 19665416 | tf_op jit(solution)/shard_map/ijab,jpb->ipa/dot_general | solution.py:43
  195.8 0.0 collective-permute-done.4
  195.8 4.5 fusion.82
  200.3 25.6 %add_bitcast_fusion = f32[1,3072,1024]{1,2,0:T(8,128)} fusion(f32[1024,3072]{1,0:T(8,128)} %fusion.135, f32[1024,3072]{1,0:T(8,128)} %fusion.138, f32[1024,3072]{1,0:T(8,128)} %fusion.141, f32[1024,3072]{1,0:T(8,128)} %fusion.131, f32[1024,3072]{1,0:T(8,128)} %fusion.144, bf16[1024,128]{0,1:T(8,128)(2,1)S(1)} %fusion.82, ...), kind=kOutput, calls=%fused_computation | convolution fusion | flops 821035008 | bytes 76546048 | tf_op jit(solution)/shard_map/ijab,jpb->ipa/dot_general | solution.py:61
  225.8 0.0 reduce-scatter.2.cloned.1.call-update
  225.9 0.9 copy-done.6
  226.8 5.1 fusion.22
  231.9 0.0 slice-start.3
  231.9 0.1 collective-permute-start.5
  232.0 122.8 %collective-permute-done.5 = f32[1,3072,128]{1,2,0:T(8,128)S(1)} collective-permute-done((f32[1,3072,128]{1,2,0:T(8,128)S(1)}, f32[1,3072,128]{1,2,0:T(8,128)S(1)}, u32[]{:S(2)}, u32[]{:S(2)}) %collective-permute-start.5) | collective-permute-done | bytes 1572896 | tf_op jit(solution)/shard_map/ppermute | solution.py:11
  354.8 5.0 fusion.37
  359.8 0.1 collective-permute-start.6
  360.0 2.2 fusion.28
  362.2 54.4 %collective-permute-done.6 = f32[1,3072,128]{1,2,0:T(8,128)S(1)} collective-permute-done((f32[1,3072,128]{1,2,0:T(8,128)S(1)}, f32[1,3072,128]{1,2,0:T(8,128)S(1)}, u32[]{:S(2)}, u32[]{:S(2)}) %collective-permute-start.6) | collective-permute-done | bytes 1572896 | tf_op jit(solution)/shard_map/ppermute | solution.py:11
  416.6 0.2 add.215
  416.8 0.1 collective-permute-start.7
  416.9 2.2 fusion.31
  419.1 53.8 %collective-permute-done.7 = f32[1,3072,128]{1,2,0:T(8,128)S(1)} collective-permute-done((f32[1,3072,128]{1,2,0:T(8,128)S(1)}, f32[1,3072,128]{1,2,0:T(8,128)S(1)}, u32[]{:S(2)}, u32[]{:S(2)}) %collective-permute-start.7) | collective-permute-done | bytes 1572896 | tf_op jit(solution)/shard_map/ppermute | solution.py:11
  473.0 0.2 add.216
  473.2 0.3 collective-permute-start.8
  473.6 2.2 fusion.34
  475.8 20.7 %collective-permute-done.8 = f32[1,3072,128]{1,2,0:T(8,128)S(1)} collective-permute-done((f32[1,3072,128]{1,2,0:T(8,128)S(1)}, f32[1,3072,128]{1,2,0:T(8,128)S(1)}, u32[]{:S(2)}, u32[]{:S(2)}) %collective-permute-start.8) | collective-permute-done | bytes 1572896 | tf_op jit(solution)/shard_map/ppermute | solution.py:11
  496.5 0.2 add.217
  496.8 0.1 collective-permute-start.9
  496.8 36.9 %collective-permute-done.9 = f32[1,3072,128]{1,2,0:T(8,128)S(1)} collective-permute-done((f32[1,3072,128]{1,2,0:T(8,128)S(1)}, f32[1,3072,128]{1,2,0:T(8,128)S(1)}, u32[]{:S(2)}, u32[]{:S(2)}) %collective-permute-start.9) | collective-permute-done | bytes 1572896 | tf_op jit(solution)/shard_map/ppermute | solution.py:11
  533.8 1.6 add.218
  535.4 1.6 copy.6
  (14 shorter events, 0.0 us)
Async XLA Ops:
  6.5 142.6 %all-gather.2.cloned.1.call-start = ((), (), s32[]{:S(2)}) async-start(), calls=%async_computation.1 | async-start | bytes 7077888 | tf_op jit(solution)/shard_map/all_gather | solution.py:39
  7.3 526.5 %reduce-scatter.2.cloned.1.call-start = ((), (), s32[]{:S(2)}) async-start(), calls=%async_computation.2 | async-start | bytes 14155776 | tf_op jit(solution)/shard_map/reduce_scatter | solution.py:78
  7.3 17.2 %collective-permute-start = (bf16[1,3072,128]{2,1,0:T(8,128)(2,1)}, bf16[1,3072,128]{2,1,0:T(8,128)(2,1)S(1)}, u32[]{:S(2)}, u32[]{:S(2)}) collective-permute-start(bf16[1,3072,128]{2,1,0:T(8,128)(2,1)} %param.5), channel_id=1, source_target_pairs={{0,8},{8,16},{16,24},{24,32},{32,40},{40,48},{48,56},{56,64},{64,7... | collective-permute-start | bytes 2359304 | tf_op jit(solution)/shard_map/ppermute | solution.py:11
  24.5 58.5 %collective-permute-start.1 = (bf16[1,3072,128]{2,1,0:T(8,128)(2,1)S(1)}, bf16[1,3072,128]{2,1,0:T(8,128)(2,1)S(1)}, u32[]{:S(2)}, u32[]{:S(2)}) collective-permute-start(bf16[1,3072,128]{2,1,0:T(8,128)(2,1)S(1)} %collective-permute-done), channel_id=1, source_target_pairs={{0,8},{8,16},{16,24},{24,32},{32,40},{40,48},{48,56},{56,64},{64,7... | collective-permute-start | bytes 2359304 | tf_op jit(solution)/shard_map/ppermute | solution.py:11
  83.1 55.2 %copy-start.1 = (bf16[1,3072,128]{2,1,0:T(8,128)(2,1)}, bf16[1,3072,128]{2,1,0:T(8,128)(2,1)S(1)}, u32[]{:S(2)}) copy-start(bf16[1,3072,128]{2,1,0:T(8,128)(2,1)S(1)} %collective-permute-done.1) | copy-start | bytes 2359300
  83.1 38.9 %collective-permute-start.2 = (bf16[1,3072,128]{2,1,0:T(8,128)(2,1)S(1)}, bf16[1,3072,128]{2,1,0:T(8,128)(2,1)S(1)}, u32[]{:S(2)}, u32[]{:S(2)}) collective-permute-start(bf16[1,3072,128]{2,1,0:T(8,128)(2,1)S(1)} %collective-permute-done.1), channel_id=1, source_target_pairs={{0,8},{8,16},{16,24},{24,32},{32,40},{40,48},{48,56},{56,64},{64,7... | collective-permute-start | bytes 2359304 | tf_op jit(solution)/shard_map/ppermute | solution.py:11
  122.0 27.1 %collective-permute-start.3 = (bf16[1,3072,128]{2,1,0:T(8,128)(2,1)S(1)}, bf16[1,3072,128]{2,1,0:T(8,128)(2,1)S(1)}, u32[]{:S(2)}, u32[]{:S(2)}) collective-permute-start(bf16[1,3072,128]{2,1,0:T(8,128)(2,1)S(1)} %collective-permute-done.2), channel_id=1, source_target_pairs={{0,8},{8,16},{16,24},{24,32},{32,40},{40,48},{48,56},{56,64},{64,7... | collective-permute-start | bytes 2359304 | tf_op jit(solution)/shard_map/ppermute | solution.py:11
  149.1 46.7 %collective-permute-start.4 = (bf16[1,3072,128]{2,1,0:T(8,128)(2,1)S(1)}, bf16[1,3072,128]{2,1,0:T(8,128)(2,1)S(1)}, u32[]{:S(2)}, u32[]{:S(2)}) collective-permute-start(bf16[1,3072,128]{2,1,0:T(8,128)(2,1)S(1)} %collective-permute-done.3), channel_id=1, source_target_pairs={{0,8},{8,16},{16,24},{24,32},{32,40},{40,48},{48,56},{56,64},{64,7... | collective-permute-start | bytes 2359304 | tf_op jit(solution)/shard_map/ppermute | solution.py:11
  149.1 5.2 copy-start.2
  149.1 11.6 %slice-start = ((s8[6291456]{0:T(1024)(128)(4,1)}), s8[4194304]{0:T(1024)(128)(4,1)S(1)}, s32[]{:S(2)}) async-start(s8[6291456]{0:T(1024)(128)(4,1)} %bitcast.250), calls=%async_computation.3 | async-start | bytes 8388608
  154.3 6.4 %slice-start.1 = ((s8[6291456]{0:T(1024)(128)(4,1)}), s8[2097152]{0:T(1024)(128)(4,1)S(1)}, s32[]{:S(2)}) async-start(s8[6291456]{0:T(1024)(128)(4,1)} %bitcast.250), calls=%async_computation.4 | async-start | bytes 4194304
  154.4 6.4 %copy-start.7 = (f32[1024]{0:T(1024)S(1)}, f32[1024]{0:T(1024)}, u32[]{:S(2)}) copy-start(f32[1024]{0:T(1024)} %param.8) | copy-start | bytes 12292
  162.4 6.3 %copy-start.5 = (bf16[1024,128]{0,1:T(8,128)(2,1)}, bf16[1024,128]{0,1:T(8,128)(2,1)S(1)}, u32[]{:S(2)}) copy-start(bf16[1024,128]{0,1:T(8,128)(2,1)S(1)} %fusion.118) | copy-start | bytes 786436
  170.4 6.5 %copy-start.3 = (bf16[1024,128]{0,1:T(8,128)(2,1)}, bf16[1024,128]{0,1:T(8,128)(2,1)S(1)}, u32[]{:S(2)}) copy-start(bf16[1024,128]{0,1:T(8,128)(2,1)S(1)} %fusion.100) | copy-start | bytes 786436
  178.5 6.3 %copy-start = (bf16[1,3072,128]{2,1,0:T(8,128)(2,1)S(1)}, bf16[1,3072,128]{2,1,0:T(8,128)(2,1)}, u32[]{:S(2)}) copy-start(bf16[1,3072,128]{2,1,0:T(8,128)(2,1)} %param.5) | copy-start | bytes 2359300
  225.8 0.9 copy-start.6
  226.8 133.2 %slice-start.2 = ((s8[6291456]{0:T(1024)(128)(4,1)}), s8[4194304]{0:T(1024)(128)(4,1)S(1)}, s32[]{:S(2)}) async-start(s8[6291456]{0:T(1024)(128)(4,1)} %bitcast.252), calls=%async_computation.5 | async-start | bytes 8388608
  231.9 128.0 %slice-start.3 = ((s8[6291456]{0:T(1024)(128)(4,1)}), s8[2097152]{0:T(1024)(128)(4,1)S(1)}, s32[]{:S(2)}) async-start(s8[6291456]{0:T(1024)(128)(4,1)} %bitcast.252), calls=%async_computation.6 | async-start | bytes 4194304
  231.9 128.0 %copy-start.4 = (bf16[1024,128]{0,1:T(8,128)(2,1)S(1)}, bf16[1024,128]{0,1:T(8,128)(2,1)}, u32[]{:S(2)}) copy-start(bf16[1024,128]{0,1:T(8,128)(2,1)} %copy-done.3) | copy-start | bytes 786436
  231.9 122.9 %collective-permute-start.5 = (f32[1,3072,128]{1,2,0:T(8,128)S(1)}, f32[1,3072,128]{1,2,0:T(8,128)S(1)}, u32[]{:S(2)}, u32[]{:S(2)}) collective-permute-start(f32[1,3072,128]{1,2,0:T(8,128)S(1)} %fusion.22), channel_id=1, source_target_pairs={{0,8},{8,16},{16,24},{24,32},{32,40},{40,48},{48,56},{56,64},{64,7... | collective-permute-start | bytes 4718600 | tf_op jit(solution)/shard_map/ppermute | solution.py:11
  359.8 56.7 %collective-permute-start.6 = (f32[1,3072,128]{1,2,0:T(8,128)S(1)}, f32[1,3072,128]{1,2,0:T(8,128)S(1)}, u32[]{:S(2)}, u32[]{:S(2)}) collective-permute-start(f32[1,3072,128]{1,2,0:T(8,128)S(1)} %fusion.37), channel_id=1, source_target_pairs={{0,8},{8,16},{16,24},{24,32},{32,40},{40,48},{48,56},{56,64},{64,7... | collective-permute-start | bytes 4718600 | tf_op jit(solution)/shard_map/ppermute | solution.py:11
  416.8 56.1 %collective-permute-start.7 = (f32[1,3072,128]{1,2,0:T(8,128)S(1)}, f32[1,3072,128]{1,2,0:T(8,128)S(1)}, u32[]{:S(2)}, u32[]{:S(2)}) collective-permute-start(f32[1,3072,128]{1,2,0:T(8,128)S(1)} %add.215), channel_id=1, source_target_pairs={{0,8},{8,16},{16,24},{24,32},{32,40},{40,48},{48,56},{56,64},{64,7... | collective-permute-start | bytes 4718600 | tf_op jit(solution)/shard_map/ppermute | solution.py:11
  473.2 23.3 %collective-permute-start.8 = (f32[1,3072,128]{1,2,0:T(8,128)S(1)}, f32[1,3072,128]{1,2,0:T(8,128)S(1)}, u32[]{:S(2)}, u32[]{:S(2)}) collective-permute-start(f32[1,3072,128]{1,2,0:T(8,128)S(1)} %add.216), channel_id=1, source_target_pairs={{0,8},{8,16},{16,24},{24,32},{32,40},{40,48},{48,56},{56,64},{64,7... | collective-permute-start | bytes 4718600 | tf_op jit(solution)/shard_map/ppermute | solution.py:11
  496.8 37.0 %collective-permute-start.9 = (f32[1,3072,128]{1,2,0:T(8,128)S(1)}, f32[1,3072,128]{1,2,0:T(8,128)S(1)}, u32[]{:S(2)}, u32[]{:S(2)}) collective-permute-start(f32[1,3072,128]{1,2,0:T(8,128)S(1)} %add.217), channel_id=1, source_target_pairs={{0,216},{8,224},{16,232},{24,240},{32,248},{40,0},{48,8},{56,16},{... | collective-permute-start | bytes 4718600 | tf_op jit(solution)/shard_map/ppermute | solution.py:11
Sparse Core Ops, SparseCore 0:
  9.0 81.4 all-gather.1
  226.0 171.0 reduce-scatter.1
where the time goes:
time: 544 us
  waiting for transfers between devices  415 us (76%)
  matrix products  93.3 us (17%)
  between operations  21.2 us (4%)
  other arithmetic  8.12 us (1%)
  local copies, waits for them, and re-layouts  5.57 us (1%)
    ppermute x10, waiting for transfers between devices, passed_along(): lax.ppermute(array, axis, [(i, (i + by) % length) for i in range(length)])  414 us
    dot_general x5, matrix products, per_device(): jnp.einsum('ijab,jpb->ipa', amplitude, visiting, preferred_element_type=j...  51 us
    dot_general x5, matrix products, per_device(): jnp.einsum('ijab,ipa->jpb', stored_amps[round_index - 1], gathered, prefe...  16.8 us
    dot_general x5, matrix products, amplitudes(): jnp.einsum('ipa,jpb->ijab', gathered, visiting, preferred_element_type=jn...  14.6 us
    dot_general x1, matrix products, per_device(): jnp.einsum('ijab,jpb->ipa', amplitude, three_index, preferred_element_typ...  11 us
  transfers between devices with their start and end apart: 12, of which 9 were waited for; matrix products, arithmetic and copies ran while one was open for 13% of the time, Pallas kernels for 0%

commit v1 on v0

v1 whole, which is shorter than its diff:
```python
import functools

import jax
import jax.numpy as jnp
from jax import lax
from jax.experimental import pallas as pl
from jax.experimental.pallas import tpu as pltpu
from jax.sharding import PartitionSpec as P

MESH = pl.DeviceIdType.MESH
F32 = jnp.float32
BF16 = jnp.bfloat16

NX, NY, NZL = 4, 4, 2
EXTRA = 16
SLOTS = 12
LN2 = 0.6931471805599453
FINE = 64.0
TOP = 32000.0
COLUMN = (0, 1, 2, 4, 6, 3, 5, 7)
RELAY = True


def scale_of(level):
    return jnp.exp(level * (LN2 / FINE))


def encode(value, ref):
    rows = value.shape[0]
    top = jnp.maximum(jnp.max(jnp.abs(value), axis=0, keepdims=True), 1e-25)
    level = jnp.ceil(jnp.log(top) * (FINE / LN2))
    factor = TOP / scale_of(level)
    ref[0:rows, :] = jnp.round(value * factor).astype(jnp.int32).astype(jnp.int16)
    spread = jnp.broadcast_to(level, (EXTRA, value.shape[1]))
    ref[rows : rows + EXTRA, :] = spread.astype(jnp.int32).astype(jnp.int16)


def decode(ref, rows):
    level = ref[rows : rows + EXTRA, :].astype(jnp.int32).astype(F32)[0:1, :]
    return ref[0:rows, :].astype(jnp.int32).astype(F32) * (scale_of(level) * (1.0 / TOP))


def kernel(n_wide, naux, nloc, omap, occ, x, xt, kept, vir, out, bs, gt, va, tt, work, ss, rr, sz, rz,
           loc_sem, w_send, w_recv, s_send, s_recv, l_send, l_recv, g_send, g_recv, r_send, r_recv, z_send, z_recv):
    wide = lax.axis_index("wide")
    narrow = lax.axis_index("narrow")
    core = wide % 2
    chip = wide // 2
    cx = chip % NX
    zh8 = wide - wide % (2 * NX)
    zl, cy = narrow // NY, narrow % NY

    def around(by):
        return (wide + by + n_wide) % n_wide

    def ringx(by):
        return zh8 + ((cx + by + NX) % NX) * 2 + core

    up, down = (around(2), narrow), (around(-2), narrow)
    sib = (wide + 1 - 2 * core, narrow)
    right = (wide, zl * NY + (cy + 1) % NY)
    left = (wide, zl * NY + (cy + NY - 1) % NY)
    zpart = (wide, (1 - zl) * NY + cy)
    zup, zdown = (around(2 * NX), narrow), (around(-2 * NX), narrow)
    xup, xdown = (ringx(1), narrow), (ringx(-1), narrow)

    half = naux // 2
    h0, h1 = pl.ds(0, half), pl.ds(half, half + EXTRA)
    halves = (h0, h1)
    own = 4 + core
    other = 5 - core

    local = [
        pltpu.make_async_copy(x, bs.at[own, pl.ds(0, naux)], loc_sem.at[0]),
        pltpu.make_async_copy(kept, bs.at[own, pl.ds(naux, EXTRA)], loc_sem.at[1]),
        pltpu.make_async_copy(xt, gt.at[0], loc_sem.at[2]),
    ]
    for c in local:
        c.start()
    barrier = pltpu.get_barrier_semaphore()
    greeted = [up, down, sib, right, left, zpart, zup, zdown, xup, xdown]
    for device in greeted:
        pl.semaphore_signal(barrier, inc=1, device_id=device, device_id_type=MESH)
    pl.semaphore_wait(barrier, len(greeted))
    for c in local:
        c.wait()

    sent = []

    def send(src, dst, s_sem, r_sem, device):
        c = pltpu.make_async_remote_copy(src_ref=src, dst_ref=dst, send_sem=s_sem, recv_sem=r_sem,
                                         device_id=device, device_id_type=MESH)
        c.start()
        return c

    def arrived(dst, r_sem):
        pltpu.make_async_remote_copy(src_ref=dst, dst_ref=dst, send_sem=g_send.at[0], recv_sem=r_sem,
                                     device_id=sib, device_id_type=MESH).wait_recv()

    edge_up = cx == NX - 1
    edge_down = cx == 0

    def hop(message, src, slot, h, device, edge, over, relay):
        part = halves[h]
        if h == 1 and RELAY:
            to = (jnp.where(edge, over[0], device[0]), narrow)
            idx = jnp.where(edge, SLOTS + relay, slot)
            sent.append(send(bs.at[src, part], bs.at[idx, part], w_send.at[message, h], w_recv.at[idx, h], to))
        else:
            sent.append(send(bs.at[src, part], bs.at[slot, part], w_send.at[message, h], w_recv.at[slot, h], device))

    def hop_up(message, src, slot, h, relay):
        hop(message, src, slot, h, up, edge_up, zup, relay)

    def hop_down(message, src, slot, h, relay):
        hop(message, src, slot, h, down, edge_down, zdown, relay)

    def relayed(index, slot_up, slot_down, up_on, down_on):
        if not RELAY:
            return
        slot = jnp.where(edge_up, slot_up, slot_down)
        to = (jnp.where(edge_up, xup[0], xdown[0]), narrow)

        @pl.when(jnp.logical_or(jnp.logical_and(edge_up, up_on), jnp.logical_and(edge_down, down_on)))
        def _():
            arrived(bs.at[SLOTS + index, h1], w_recv.at[SLOTS + index, 1])
            send(bs.at[SLOTS + index, h1], bs.at[slot, h1], l_send.at[index], w_recv.at[slot, 1], to)

    def relay_done(index, up_on, down_on):
        if not RELAY:
            return

        @pl.when(jnp.logical_or(jnp.logical_and(edge_up, up_on), jnp.logical_and(edge_down, down_on)))
        def _():
            part = bs.at[SLOTS + index, h1]
            pltpu.make_async_remote_copy(src_ref=part, dst_ref=part, send_sem=l_send.at[index], recv_sem=w_recv.at[SLOTS + index, 1],
                                         device_id=sib, device_id_type=MESH).wait_send()

    def take(slot, h):
        arrived(bs.at[slot, halves[h]], w_recv.at[slot, h])

    def share(index, slot):
        sent.append(send(bs.at[slot], bs.at[slot], s_send.at[index], s_recv.at[slot], sib))

    def shared(slot):
        arrived(bs.at[slot], s_recv.at[slot])

    lo, hi = pl.ds(0, nloc // 2), pl.ds(nloc // 2, nloc // 2)

    sent.append(send(gt.at[0], gt.at[1], g_send.at[0], g_recv.at[1, 0], zpart))
    sent.append(send(gt.at[0], gt.at[3], g_send.at[1], g_recv.at[3, 0], right))
    sent.append(send(gt.at[0], gt.at[2], g_send.at[2], g_recv.at[2, 0], left))
    hop_up(0, own, 2 + core, 0, 0)
    hop_down(1, own, 6 + core, 0, 0)
    hop_up(0, own, 2 + core, 1, 0)
    hop_down(1, own, 6 + core, 1, 0)
    share(0, own)

    gy = (0, 0, 1, 3, 2, 1, 3, 2)
    gz = (0, 1, 0, 0, 0, 1, 1, 1)
    for g in range(8):
        row = vir[pl.ds(((zl + gz[g]) % NZL) * NY + (cy + gy[g]) % NY, 1), :]
        va[g] = jnp.broadcast_to(row, (nloc, nloc)).T
    vb = vir[pl.ds(narrow, 1), :]
    e_own = occ[omap[wide]]
    rows16 = lax.broadcasted_iota(jnp.int32, (EXTRA, nloc), 0)

    def block(q, g0, ng):
        pair = jnp.concatenate([bs[2 * q, 0:naux, :], bs[2 * q + 1, 0:naux, :]], axis=1)
        a = gt[g0 : g0 + ng].reshape(ng * nloc, naux)
        work[0 : ng * nloc, :] = jnp.dot(a, pair, preferred_element_type=F32)
        mine = bs[own, naux : naux + EXTRA, :].astype(F32)
        for k in range(2):
            j_off = jnp.where(q == 5, 6 - 11 * k, 2 * (q - 2) + k)
            e_sum = e_own + occ[omap[around(2 * chip - wide + j_off)]]
            delta = core - j_off
            theirs = bs[2 * q + k, naux : naux + EXTRA, :].astype(F32)
            pick = jnp.where(delta >= 0, mine, theirs)
            w = jnp.sum(jnp.where(rows16 == jnp.abs(delta), pick, 0.0), axis=0, keepdims=True)
            for g in range(g0, g0 + ng):
                v = work[(g - g0) * nloc : (g - g0 + 1) * nloc, k * nloc : (k + 1) * nloc]
                t = w * v / ((va[g] + vb) - e_sum)
                tt[pl.ds((2 * q + k) * nloc, nloc), COLUMN[g] * nloc : (COLUMN[g] + 1) * nloc] = t.T.astype(BF16)

    def blocks(first, count, stride, g0, ng):
        @pl.loop(0, count)
        def _(i):
            block(first + i * stride, g0, ng)

    shared(other)

    take(2 + core, 0)
    hop_up(2, 2 + core, core, 0, 1)
    take(6 + core, 0)
    hop_down(3, 6 + core, 8 + core, 0, 1)
    relayed(0, 2 + core, 6 + core, True, True)
    take(2 + core, 1)
    hop_up(2, 2 + core, core, 1, 1)
    share(1, 2 + core)
    take(6 + core, 1)
    hop_down(3, 6 + core, 8 + core, 1, 1)
    share(2, 6 + core)

    arrived(gt.at[3], g_recv.at[3, 0])
    sent.append(send(gt.at[3, lo], gt.at[4, lo], g_send.at[3], g_recv.at[4, 0], right))
    arrived(gt.at[2], g_recv.at[2, 0])
    sent.append(send(gt.at[2, hi], gt.at[4, hi], g_send.at[4], g_recv.at[4, 1], left))
    arrived(gt.at[1], g_recv.at[1, 0])
    sent.append(send(gt.at[1], gt.at[6], g_send.at[5], g_recv.at[6, 0], right))
    sent.append(send(gt.at[1], gt.at[5], g_send.at[6], g_recv.at[5, 0], left))

    shared(3 - core)
    shared(7 - core)
    blocks(1, 3, 1, 0, 4)

    third_src = 8 - 7 * core
    third_to = jnp.where(core == 0, down[0], up[0])
    third_over = jnp.where(core == 0, zdown[0], zup[0])
    third_edge = jnp.logical_or(jnp.logical_and(core == 0, edge_down), jnp.logical_and(core == 1, edge_up))
    take(core, 0)
    take(8 + core, 0)
    hop(4, third_src, 10 + core, 0, (third_to, narrow), third_edge, (third_over, narrow), 2)
    relayed(1, core, 8 + core, True, True)
    take(core, 1)
    take(8 + core, 1)
    hop(4, third_src, 10 + core, 1, (third_to, narrow), third_edge, (third_over, narrow), 2)
    share(3, core)
    share(4, 8 + core)

    arrived(gt.at[4, lo], g_recv.at[4, 0])
    arrived(gt.at[4, hi], g_recv.at[4, 1])
    shared(1 - core)
    shared(9 - core)
    blocks(1, 3, 1, 4, 1)

    arrived(gt.at[6], g_recv.at[6, 0])
    sent.append(send(gt.at[6, lo], gt.at[7, lo], g_send.at[7], g_recv.at[7, 0], right))
    arrived(gt.at[5], g_recv.at[5, 0])
    sent.append(send(gt.at[5, hi], gt.at[7, hi], g_send.at[8], g_recv.at[7, 1], left))
    blocks(0, 2, 4, 0, 7)
    relayed(2, 10 + core, 10 + core, core == 1, core == 0)
    take(10 + core, 0)
    take(10 + core, 1)
    share(5, 10 + core)
    blocks(1, 3, 1, 5, 2)
    shared(11 - core)
    blocks(5, 1, 1, 0, 7)
    arrived(gt.at[7, lo], g_recv.at[7, 0])
    arrived(gt.at[7, hi], g_recv.at[7, 1])
    blocks(0, 6, 1, 7, 1)

    quarter = naux // 4

    def tile(p, part):
        r0 = pl.multiple_of(part * quarter, quarter)
        lhs = jnp.concatenate([bs[s, pl.ds(r0, quarter), :] for s in range(SLOTS)], axis=1)
        cols = pl.ds(pl.multiple_of(p * 2 * nloc, 2 * nloc), 2 * nloc)
        work[0:quarter, :] = jnp.dot(lhs, tt[:, cols], preferred_element_type=F32)

    def y_copy(t):
        way, stage, j = t % 2, t // 4, (t % 4) // 2
        part = jnp.where(stage == 1, (1 - way) * 2 + j, way * 2 + j)
        slot = jnp.where(stage == 0, way * 2 + j, 4 + way * 4 + part)
        to = (wide, jnp.where(way == 0, right[1], left[1]))
        c = pltpu.make_async_remote_copy(src_ref=ss.at[t], dst_ref=rr.at[slot], send_sem=r_send.at[t], recv_sem=r_recv.at[slot],
                                         device_id=to, device_id_type=MESH)
        return c, way, stage, part, slot

    @pl.loop(0, 12)
    def _(t):
        c, way, stage, part, _ = y_copy(t)
        tile(jnp.where(stage == 0, 3, 1 + way), part)

        @pl.when(stage == 2)
        def _():
            arrived(rr.at[part], r_recv.at[part])
            work[0:quarter, :] += decode(rr.at[part], quarter)

        encode(work[0:quarter, :], ss.at[t])
        c.start()

    def z_copy(part):
        return pltpu.make_async_remote_copy(src_ref=sz.at[part], dst_ref=rz.at[part], send_sem=z_send.at[part], recv_sem=z_recv.at[part],
                                            device_id=zpart, device_id_type=MESH)

    @pl.loop(0, 4)
    def _(t):
        part = (t % 2) * 2 + t // 2
        tile(0, part)
        arrived(rr.at[4 + part], r_recv.at[4 + part])
        arrived(rr.at[8 + part], r_recv.at[8 + part])
        total = work[0:quarter, :] + decode(rr.at[4 + part], quarter) + decode(rr.at[8 + part], quarter)
        out[pl.ds(pl.multiple_of(part * quarter, quarter), quarter), :] = total[:, 0:nloc]
        encode(total[:, nloc : 2 * nloc], sz.at[part])
        z_copy(part).start()

    @pl.loop(0, 4)
    def _(t):
        part = (t % 2) * 2 + t // 2
        z_copy(part).wait_recv()
        out[pl.ds(pl.multiple_of(part * quarter, quarter), quarter), :] += decode(rz.at[part], quarter)

    for c in sent:
        c.wait_send()
    relay_done(0, True, True)
    relay_done(1, True, True)
    relay_done(2, core == 1, core == 0)

    @pl.loop(0, 12)
    def _(t):
        y_copy(t)[0].wait_send()

    @pl.loop(0, 4)
    def _(t):
        z_copy(t).wait_send()


def per_device(three_index, orbital_map, occ_energy, vir_energy, pair_kept):
    _, naux, nloc = three_index.shape
    n_wide = lax.axis_size("wide")
    n_narrow = lax.axis_size("narrow")
    x = three_index.reshape(naux, nloc)
    kept = jnp.pad(pair_kept, ((0, EXTRA - pair_kept.shape[0]), (0, 0))).astype(BF16)
    kept = jnp.broadcast_to(kept, (EXTRA, nloc))
    vir = vir_energy.reshape(n_narrow, nloc)
    quarter = naux // 4
    vmem = functools.partial(pl.BlockSpec, memory_space=pltpu.VMEM)
    smem = functools.partial(pl.BlockSpec, memory_space=pltpu.SMEM)
    hbm = functools.partial(pl.BlockSpec, memory_space=pl.ANY)
    dma = pltpu.SemaphoreType.DMA
    density = pl.pallas_call(
        functools.partial(kernel, n_wide, naux, nloc),
        out_shape=jax.ShapeDtypeStruct((naux, nloc), F32),
        in_specs=[smem(), smem(), hbm(), hbm(), hbm(), vmem()],
        out_specs=vmem(),
        scratch_shapes=[
            pltpu.VMEM((SLOTS + 3, naux + EXTRA, nloc), BF16),
            pltpu.VMEM((8, nloc, naux), BF16),
            pltpu.VMEM((8, nloc, nloc), F32),
            pltpu.VMEM((SLOTS * nloc, 8 * nloc), BF16),
            pltpu.VMEM((7 * nloc, 2 * nloc), F32),
            pltpu.VMEM((12, quarter + EXTRA, 2 * nloc), jnp.int16),
            pltpu.VMEM((12, quarter + EXTRA, 2 * nloc), jnp.int16),
            pltpu.VMEM((4, quarter + EXTRA, nloc), jnp.int16),
            pltpu.VMEM((4, quarter + EXTRA, nloc), jnp.int16),
            dma((3,)),
            dma((5, 2)),
            dma((SLOTS + 3, 2)),
            dma((6,)),
            dma((SLOTS,)),
            dma((3,)),
            dma((3,)),
            dma((9,)),
            dma((8, 2)),
            dma((12,)),
            dma((12,)),
            dma((4,)),
            dma((4,)),
        ],
        compiler_params=pltpu.CompilerParams(
            collective_id=0, has_side_effects=True, vmem_limit_bytes=60 * 1024 * 1024
        ),
    )(orbital_map, occ_energy, x, x.T, kept, vir)
    return density.reshape(1, naux, nloc)


def solution(mesh):
    placed = (P("wide", None, "narrow"), P(), P(), P(), P(None, "wide"))
    return jax.shard_map(
        per_device, mesh=mesh, in_specs=placed, out_specs=P("wide", None, "narrow"), check_vma=False
    )
```

time: 544 us -> 208 us (0.38)
  the two profiles are of different devices: /device:TPU:64 before, /device:TPU:7 now
where the time goes in v1:
time: 208 us; the launch traced here: 205 us
  Pallas kernels  199 us (96%)
  local copies, waits for them, and re-layouts  5.61 us (3%)
    pallas_call x1, Pallas kernels, per_device(): pl.pallas_call(functools.partial(kernel, n_wide, naux, nloc), out_shape=j...  199 us
    unnamed x2, local copies, waits for them, and re-layouts  4.94 us

profile of v1, /device:TPU:7, one launch (start us, length us, event | category | flops | bytes accessed | tf_op | source)
XLA Modules:
  0.0 205.1 jit_solution(16662463878382798724)
XLA Ops:
  0.0 0.7 convert.4
  0.7 0.7 broadcast_in_dim.8.kept
  1.3 2.3 %copy.6 = bf16[1,3072,128]{1,2,0:T(8,128)(2,1)} copy(bf16[1,3072,128]{2,1,0:T(8,128)(2,1)} %param.5) | data formatting | bytes 1572864 | tf_op args[0]
  3.6 198.8 %shard_map.55 = f32[3072,128]{1,0:T(8,128)} custom-call(s32[32]{0:T(128)} %omap.1, f32[32]{0:T(128)} %occ.1, bf16[3072,128]{1,0:T(8,128)(2,1)} %bitcast.9, bf16[128,3072]{1,0:T(8,128)(2,1)} %bitcast.10, bf16[16,128]{1,0:T(8,128)(2,1)} %broadcast_in_dim.8.kept, f32[8,128]{1,0:T(8,128)} %bitcast.11), custom_call_target="tpu_custom_call" | custom-call | tf_op jit(solution)/shard_map/pallas_call | solution.py:331
  202.4 2.7 %copy.10 = f32[1,3072,128]{2,1,0:T(8,128)} copy(f32[1,3072,128]{2,1,0:T(8,128)} %bitcast.8) | data formatting | bytes 3145728
  (1 shorter events, 0.0 us)

commit v2 on v1

v2 whole, which is shorter than its diff:
```python
import functools
import heapq

import jax
import jax.numpy as jnp
from jax import lax
from jax.experimental import pallas as pl
from jax.experimental.pallas import tpu as pltpu
from jax.sharding import PartitionSpec as P

MESH = pl.DeviceIdType.MESH
F32 = jnp.float32
BF16 = jnp.bfloat16

NX, NY, NZL = 4, 4, 2
EXTRA = 16
SLOTS = 12
LN2 = 0.6931471805599453
FINE = 64.0
TOP = 32000.0
COLUMN = (0, 2, 4, 6, 1, 3, 5, 7)

HOP = 0.2
ROUTES = {
    (3, 1): ((3, ((3, 0), (0, 1), (3, 2))),),
    (3, 0): ((0, ((0, 1),)),),
    (2, 1): ((1, ((1, 0),)),),
    (2, 0): ((2, ((2, 1), (1, 0))),),
    (1, 1): ((1, ((1, 0),)), (0, ())),
}
ORDER = ((2, 3, 4, 5, 1, 0), (1, 2, 3, 4, 5, 0), (1, 2, 3, 0, 5, 4), (0, 1, 2, 5, 3, 4))
PHASES = ((3, 3), (4, 5), (5, 5), (5, 7), (6, 7), (6, 8))
RELAYS = 2


def slot_of(x, k, dz, owner):
    off = NX * dz + owner - x
    if -2 <= off <= 2:
        return 2 * (off + 2) + k
    if off == 3 and k == 0:
        return 10
    if off == -3 and k == 1:
        return 11
    return None


def messages():
    out = []

    def fw(k, xs, xd, dz, owner, h, rank=1):
        xs, xd, owner = xs % NX, xd % NX, owner % NX
        kind = "x+" if (xs + 1) % NX == xd else "x-"
        out.append((("S", dz, owner, h), kind, xs, xd, k, ("S", dz, owner, h), rank))

    for k in (0, 1):
        for x in range(NX):
            for h in (0, 1):
                fw(k, x, x + 1, 0, x, h, 2 + 0.1 * h)
                fw(k, x, x - 1, 0, x, 1 - h, 2 + 0.1 * h)
            fw(k, x + 1, x + 2, 0, x, 0)
            fw(k, x - 1, x - 2, 0, x, 1)
        for up in (True, False):
            kk, dz = (k, -1) if up else (1 - k, 1)

            def m(v, up=up):
                return v if up else NX - 1 - v

            for (owner, odd), ways in ROUTES.items():
                for h in (0, 1) if odd == k else ():
                    column, edges = ways[h * len(ways) // 2]
                    g = h if up else 1 - h
                    sent, got = ("S", 0, m(owner), g), ("S", dz, m(owner), g)
                    out.append((sent, "z+" if up else "z-", m(column), m(column), kk, got, 1))
                    for xs, xd in edges:
                        fw(kk, m(xs), m(xd), dz, m(owner), g, 0)
        for x in range(NX):

            def ag(g0, kind, g1, h, rank, k=k, x=x):
                out.append((("A", g0, h), kind, x, x, k, ("A", g1, h), rank))

            for h in (0, 1):
                ag(0, "zz", 4, h, 1 + 0.1 * h)
                ag(0, "y+", 2, h, 2 + 0.1 * h)
                ag(0, "y-", 1, 1 - h, 2 + 0.1 * h)
                ag(4, "y+", 6, h, 3)
                ag(4, "y-", 5, 1 - h, 3)
            ag(2, "y+", 3, 0, 1)
            ag(1, "y-", 3, 1, 1)
            ag(6, "y+", 7, 0, 1)
            ag(5, "y-", 7, 1, 1)
    return out


@functools.cache
def programs():
    ms = messages()
    need, free, heap = {}, {}, []
    ops = {(x, k): [] for x in range(NX) for k in (0, 1)}
    have, ready, late = {}, {}, {}

    def got(x, k, z, item, t):
        assert (x, k, z, item) not in late
        late[x, k, z, item] = t
        have[x, k, item] = max(have.get((x, k, item), 0.0), t)
        for i in need.get((x, k, item), ()):
            heapq.heappush(heap, (t, ms[i][6], i, z))

    for i, m in enumerate(ms):
        need.setdefault((m[2], m[4], m[0]), []).append(i)
    for x in range(NX):
        for k in (0, 1):
            for z in (0, 1):
                for h in (0, 1):
                    got(x, k, z, ("S", 0, x, h), 0.0)
                    got(x, k, z, ("A", 0, h), 0.0)
            ops[x, k].append((0.0, 9, 0, "share", 4 + k))
    while heap:
        t, rank, i, z = heapq.heappop(heap)
        _, kind, xs, xd, k, item2, _ = ms[i]
        if kind == "zz":
            links = [("even", z, xs)]
        elif kind in ("z+", "z-"):
            way = 0 if kind == "z+" else 1
            links = [("even", way, xs), ("odd", way, xs)]
        else:
            links = [(kind, xs, z)]
        start = max([t] + [free.get(link, 0.0) for link in links])
        for link in links:
            free[link] = start + 0.5
        ready[i] = max(ready.get(i, 0.0), t)
        got(xd, k, 1 - z if kind == "zz" else z, item2, start + 0.5 + HOP * len(links))
    for i, (item, kind, xs, xd, k, item2, rank) in enumerate(ms):
        ops[xs, k].append((ready[i], rank, i, "send", item, kind, xd, item2))
        ops[xd, k].append((have[xd, k, item2], -1, i, "wait", item2))
    for (x, k), program in ops.items():
        for dz in (-1, 0, 1):
            for owner in range(NX):
                both = [have.get((x, k, ("S", dz, owner, h))) for h in (0, 1)]
                slot = slot_of(x, k, dz, owner)
                if slot is not None and slot != 4 + k:
                    program.append((max(both), 1, 0, "share", slot))
        program.sort(key=lambda op: op[:3])
    return ops


@functools.cache
def phase_ends(x, k):
    ends, end = [], 0.01
    for pairs, slices in PHASES:
        slots = [2 * q + c for q in ORDER[x][:pairs] for c in (0, 1)]
        for core in (0, 1):
            for op in programs()[x, core]:
                if op[3] == "share" and op[4] in slots:
                    end = max(end, op[0])
                if op[3] == "wait" and op[4][0] == "A" and core == k and op[4][1] < slices:
                    end = max(end, op[0])
        ends.append(end)
    return [0.01, *ends, 1000.0]


def places(x, k):
    found, spare = {}, SLOTS
    for op in programs()[x, k]:
        if op[3] == "wait" and op[4][0] == "S" and op[4][:3] not in found:
            slot = slot_of(x, k, op[4][1], op[4][2])
            if slot is None:
                slot, spare = spare, spare + 1
            found[op[4][:3]] = slot
    found["S", 0, x] = 4 + k
    assert spare <= SLOTS + RELAYS
    return found


def scale_of(level):
    return jnp.exp(level * (LN2 / FINE))


def encode(value, ref):
    rows = value.shape[0]
    top = jnp.maximum(jnp.max(jnp.abs(value), axis=0, keepdims=True), 1e-25)
    level = jnp.ceil(jnp.log(top) * (FINE / LN2))
    factor = TOP / scale_of(level)
    ref[0:rows, :] = jnp.round(value * factor).astype(jnp.int32).astype(jnp.int16)
    spread = jnp.broadcast_to(level, (EXTRA, value.shape[1]))
    ref[rows : rows + EXTRA, :] = spread.astype(jnp.int32).astype(jnp.int16)


def decode(ref, rows):
    level = ref[rows : rows + EXTRA, :].astype(jnp.int32).astype(F32)[0:1, :]
    return ref[0:rows, :].astype(jnp.int32).astype(F32) * (scale_of(level) * (1.0 / TOP))


def kernel(n_wide, naux, nloc, omap, occ, x, xt, kept, vir, out, bs, gt, va, tt, work, keep, sy, ry, sn, rn,
           loc_sem, w_send, w_recv, s_send, s_recv, g_recv, sy_sem, ry_sem, sn_sem, rn_sem):
    wide = lax.axis_index("wide")
    narrow = lax.axis_index("narrow")
    core = wide % 2
    chip = wide // 2
    cx = chip % NX
    zh8 = wide - wide % (2 * NX)
    zl, cy = narrow // NY, narrow % NY

    def around(by):
        return (wide + by + n_wide) % n_wide

    def ringx(by):
        return zh8 + ((cx + by + NX) % NX) * 2 + core

    sib = (wide + 1 - 2 * core, narrow)
    right = (wide, zl * NY + (cy + 1) % NY)
    left = (wide, zl * NY + (cy + NY - 1) % NY)
    zpart = (wide, (1 - zl) * NY + cy)
    zup, zdown = (around(2 * NX), narrow), (around(-2 * NX), narrow)
    xup, xdown = (ringx(1), narrow), (ringx(-1), narrow)
    to = {"x+": xup, "x-": xdown, "z+": zup, "z-": zdown, "zz": zpart, "y+": right, "y-": left}

    half = naux // 2
    halves = (pl.ds(0, half), pl.ds(half, half + EXTRA))
    lo_hi = (pl.ds(0, nloc // 2), pl.ds(nloc // 2, nloc // 2))
    own = 4 + core

    local = [
        pltpu.make_async_copy(x, bs.at[own, pl.ds(0, naux)], loc_sem.at[0]),
        pltpu.make_async_copy(kept, bs.at[own, pl.ds(naux, EXTRA)], loc_sem.at[1]),
        pltpu.make_async_copy(xt, gt.at[0], loc_sem.at[2]),
    ]
    for c in local:
        c.start()
    barrier = pltpu.get_barrier_semaphore()
    greeted = [sib, *to.values()]
    for device in greeted:
        pl.semaphore_signal(barrier, inc=1, device_id=device, device_id_type=MESH)
    pl.semaphore_wait(barrier, len(greeted))
    for c in local:
        c.wait()

    def remote(src, dst, s_sem, r_sem, device):
        return pltpu.make_async_remote_copy(src_ref=src, dst_ref=dst, send_sem=s_sem, recv_sem=r_sem,
                                            device_id=device, device_id_type=MESH)

    def arrived(dst, r_sem):
        remote(dst, dst, w_send.at[0], r_sem, sib).wait_recv()

    def view(item, place):
        if item[0] == "S":
            slot, h = place[item[:3]], item[3]
            return bs.at[slot, halves[h]], w_recv.at[slot, h]
        return gt.at[item[1], lo_hi[item[2]]], g_recv.at[item[1], item[2]]

    def run(phase, finish=False):
        for x in range(NX):
            for k in (0, 1):

                @pl.when(jnp.logical_and(cx == x, core == k))
                def _(x=x, k=k):
                    place, n_sent, n_shared = places(x, k), 0, 0
                    ends = [-1.0, *phase_ends(x, k)]
                    for op in programs()[x, k]:
                        now = not finish and ends[phase] < op[0] <= ends[phase + 1]
                        if op[3] == "wait":
                            if now:
                                arrived(*view(op[4], place))
                        elif op[3] == "share":
                            part = bs.at[op[4]]
                            if now:
                                remote(part, part, s_send.at[n_shared], s_recv.at[op[4]], sib).start()
                            if finish:
                                remote(part, part, s_send.at[n_shared], s_recv.at[op[4]], sib).wait_send()
                            n_shared += 1
                        else:
                            _, _, _, _, item, kind, xd, there = op
                            dst, r_sem = view(there, places(xd, k))
                            if now:
                                remote(view(item, place)[0], dst, w_send.at[n_sent], r_sem, to[kind]).start()
                            if finish:
                                remote(view(item, place)[0], dst, w_send.at[n_sent], r_sem, to[kind]).wait_send()
                            n_sent += 1

    def shared(slot):
        arrived(bs.at[slot], s_recv.at[slot])

    run(0)

    gy = (0, 1, 3, 2) * 2
    gz = (0,) * 4 + (1,) * 4
    for g in range(8):
        row = vir[pl.ds(((zl + gz[g]) % NZL) * NY + (cy + gy[g]) % NY, 1), :]
        va[g] = jnp.broadcast_to(row, (nloc, nloc)).T
    vb = vir[pl.ds(narrow, 1), :]
    e_own = occ[omap[wide]]
    rows16 = lax.broadcasted_iota(jnp.int32, (EXTRA, nloc), 0)

    def block(q, g0, ng):
        pair = jnp.concatenate([bs[2 * q, 0:naux, :], bs[2 * q + 1, 0:naux, :]], axis=1)
        a = gt[g0 : g0 + ng].reshape(ng * nloc, naux)
        work[0 : ng * nloc, :] = jnp.dot(a, pair, preferred_element_type=F32)
        mine = bs[own, naux : naux + EXTRA, :].astype(F32)
        for k in range(2):
            j_off = jnp.where(q == 5, 6 - 11 * k, 2 * (q - 2) + k)
            e_sum = e_own + occ[omap[around(2 * chip - wide + j_off)]]
            delta = core - j_off
            theirs = bs[2 * q + k, naux : naux + EXTRA, :].astype(F32)
            pick = jnp.where(delta >= 0, mine, theirs)
            w = jnp.sum(jnp.where(rows16 == jnp.abs(delta), pick, 0.0), axis=0, keepdims=True)
            for g in range(g0, g0 + ng):
                v = work[(g - g0) * nloc : (g - g0 + 1) * nloc, k * nloc : (k + 1) * nloc]
                t = w * v / ((va[g] + vb) - e_sum)
                tt[pl.ds((2 * q + k) * nloc, nloc), COLUMN[g] * nloc : (COLUMN[g] + 1) * nloc] = t.T.astype(BF16)

    def pair_at(i):
        q = 0
        for x in range(NX):
            for j, value in enumerate(ORDER[x]):
                q = jnp.where(jnp.logical_and(cx == x, i == j), value, q)
        return q

    def blocks(first, last, g0, ng, wait=False):
        @pl.loop(first, last)
        def _(i):
            q = pair_at(i)
            if wait:
                shared(2 * q + 1 - core)
            block(q, g0, ng)

    run(1)
    blocks(0, 3, 0, 3, True)
    run(2)
    blocks(0, 3, 3, 2)
    blocks(3, 4, 0, 5, True)
    run(3)
    blocks(4, 5, 0, 5, True)
    run(4)
    blocks(0, 5, 5, 2)
    run(5)
    blocks(5, 6, 0, 7, True)
    run(6)
    run(7)
    blocks(0, 6, 7, 1)

    quarter = naux // 4

    def rows_of(part):
        return pl.ds(pl.multiple_of(part * quarter, quarter), quarter)

    def tile(p, part):
        lhs = jnp.concatenate([bs[s, rows_of(part), :] for s in range(SLOTS)], axis=1)
        cols = pl.ds(pl.multiple_of(p * 2 * nloc, 2 * nloc), 2 * nloc)
        work[0:quarter, :] = jnp.dot(lhs, tt[:, cols], preferred_element_type=F32)

    def beside(way):
        return (wide, jnp.where(way == 0, right[1], left[1]))

    def y_copy(i, way):
        return remote(sy.at[i], ry.at[i], sy_sem.at[i], ry_sem.at[i], beside(way))

    def n_copy(i, device):
        return remote(sn.at[i], rn.at[i], sn_sem.at[i], rn_sem.at[i], device)

    def took_y(i):
        arrived(ry.at[i], ry_sem.at[i])
        return decode(ry.at[i], quarter)

    def took_n(i):
        arrived(rn.at[i], rn_sem.at[i])
        return decode(rn.at[i], quarter)

    def y_step(stage):
        @pl.loop(0, 2)
        def _(way):
            tile(3 if stage == 0 else 1 + way, 1 - way if stage == 1 else way)
            value = work[0:quarter, :]
            if stage == 2:
                value = value + took_y(way)
            encode(value, sy.at[2 * stage + way])
            y_copy(2 * stage + way, way).start()

    def z_step(p):
        @pl.loop(0, 2)
        def _(j):
            tile(p, 2 + j)
            keep[2 * p + j] = work[0:quarter, 0:nloc]
            encode(work[0:quarter, nloc : 2 * nloc], sn.at[2 * p + j])
            n_copy(2 * p + j, zpart).start()

    def n_step(stage):
        @pl.loop(0, 2)
        def _(way):
            i = 6 + way if stage == 0 else 2 * (1 + way) + (1 - way if stage == 1 else way)
            value = keep[i] + took_n(i)
            if stage == 2:
                value = value + took_n(8 + way)
            encode(value, sn.at[8 + 2 * stage + way])
            n_copy(8 + 2 * stage + way, beside(way)).start()

    y_step(0)
    z_step(3)
    y_step(1)
    z_step(1)
    y_step(2)
    z_step(2)
    n_step(0)
    z_step(0)
    n_step(1)

    @pl.loop(0, 2)
    def _(part):
        tile(0, part)
        total = work[0:quarter, :] + took_y(4 - 2 * part) + took_y(3 + 2 * part)
        out[rows_of(part), :] = total[:, 0:nloc]
        encode(total[:, nloc : 2 * nloc], sn.at[14 + part])
        n_copy(14 + part, zpart).start()

    n_step(2)

    @pl.loop(0, 2)
    def _(j):
        out[rows_of(2 + j), :] = keep[j] + took_n(j) + took_n(12 - 2 * j) + took_n(11 + 2 * j)

    @pl.loop(0, 2)
    def _(part):
        out[rows_of(part), :] += took_n(14 + part)

    run(0, True)

    @pl.loop(0, 6)
    def _(i):
        y_copy(i, i % 2).wait_send()

    @pl.loop(0, 16)
    def _(i):
        n_copy(i, sib).wait_send()


def per_device(three_index, orbital_map, occ_energy, vir_energy, pair_kept):
    _, naux, nloc = three_index.shape
    n_wide = lax.axis_size("wide")
    n_narrow = lax.axis_size("narrow")
    x = three_index.reshape(naux, nloc)
    kept = jnp.pad(pair_kept, ((0, EXTRA - pair_kept.shape[0]), (0, 0))).astype(BF16)
    kept = jnp.broadcast_to(kept, (EXTRA, nloc))
    vir = vir_energy.reshape(n_narrow, nloc)
    quarter = naux // 4
    vmem = functools.partial(pl.BlockSpec, memory_space=pltpu.VMEM)
    smem = functools.partial(pl.BlockSpec, memory_space=pltpu.SMEM)
    hbm = functools.partial(pl.BlockSpec, memory_space=pl.ANY)
    dma = pltpu.SemaphoreType.DMA
    density = pl.pallas_call(
        functools.partial(kernel, n_wide, naux, nloc),
        out_shape=jax.ShapeDtypeStruct((naux, nloc), F32),
        in_specs=[smem(), smem(), hbm(), hbm(), hbm(), vmem()],
        out_specs=vmem(),
        scratch_shapes=[
            pltpu.VMEM((SLOTS + RELAYS, naux + EXTRA, nloc), BF16),
            pltpu.VMEM((8, nloc, naux), BF16),
            pltpu.VMEM((8, nloc, nloc), F32),
            pltpu.VMEM((SLOTS * nloc, 8 * nloc), BF16),
            pltpu.VMEM((8 * nloc, 2 * nloc), F32),
            pltpu.VMEM((8, quarter, nloc), F32),
            pltpu.VMEM((6, quarter + EXTRA, 2 * nloc), jnp.int16),
            pltpu.VMEM((6, quarter + EXTRA, 2 * nloc), jnp.int16),
            pltpu.VMEM((16, quarter + EXTRA, nloc), jnp.int16),
            pltpu.VMEM((16, quarter + EXTRA, nloc), jnp.int16),
            dma((3,)),
            dma((32,)),
            dma((SLOTS + RELAYS, 2)),
            dma((6,)),
            dma((SLOTS,)),
            dma((8, 2)),
            dma((6,)),
            dma((6,)),
            dma((16,)),
            dma((16,)),
        ],
        compiler_params=pltpu.CompilerParams(
            collective_id=0, has_side_effects=True, vmem_limit_bytes=60 * 1024 * 1024
        ),
    )(orbital_map, occ_energy, x, x.T, kept, vir)
    return density.reshape(1, naux, nloc)


def solution(mesh):
    placed = (P("wide", None, "narrow"), P(), P(), P(), P(None, "wide"))
    return jax.shard_map(
        per_device, mesh=mesh, in_specs=placed, out_specs=P("wide", None, "narrow"), check_vma=False
    )
```

time: 208 us -> 136 us (0.65); the launches traced: 205 us -> 136 us
  Pallas kernels: 199 us -> 130 us
    pallas_call x1, Pallas kernels: 199 us -> 130 us  [per_device(): pl.pallas_call(functools.partial(kernel, n_wide, naux, nloc), out_shape=j...]
where the time goes in v2:
time: 136 us
  Pallas kernels  130 us (96%)
  local copies, waits for them, and re-layouts  5.61 us (4%)
    pallas_call x1, Pallas kernels, per_device(): pl.pallas_call(functools.partial(kernel, n_wide, naux, nloc), out_shape=j...  130 us
    unnamed x2, local copies, waits for them, and re-layouts  4.94 us

profile of v2, /device:TPU:7, one launch (start us, length us, event | category | flops | bytes accessed | tf_op | source)
XLA Modules:
  0.0 135.8 jit_solution(3380231064706940808)
XLA Ops:
  0.0 0.7 convert.4
  0.7 0.7 broadcast_in_dim.8.kept
  1.3 2.3 %copy.6 = bf16[1,3072,128]{1,2,0:T(8,128)(2,1)} copy(bf16[1,3072,128]{2,1,0:T(8,128)(2,1)} %param.5) | data formatting | bytes 1572864 | tf_op args[0]
  3.6 129.5 %shard_map.55 = f32[3072,128]{1,0:T(8,128)} custom-call(s32[32]{0:T(128)} %omap.1, f32[32]{0:T(128)} %occ.1, bf16[3072,128]{1,0:T(8,128)(2,1)} %bitcast.9, bf16[128,3072]{1,0:T(8,128)(2,1)} %bitcast.10, bf16[16,128]{1,0:T(8,128)(2,1)} %broadcast_in_dim.8.kept, f32[8,128]{1,0:T(8,128)} %bitcast.11), custom_call_target="tpu_custom_call" | custom-call | tf_op jit(solution)/shard_map/pallas_call | solution.py:447
  133.1 2.7 %copy.10 = f32[1,3072,128]{2,1,0:T(8,128)} copy(f32[1,3072,128]{2,1,0:T(8,128)} %bitcast.8) | data formatting | bytes 3145728
  (1 shorter events, 0.0 us)

commit v3 on v2

--- a/solution.py
+++ b/solution.py
@@ -1,3 +1,4 @@
+import collections
 import functools
 import heapq
 
@@ -94,41 +95,45 @@
 @functools.cache
 def programs():
     ms = messages()
-    need, free, heap = {}, {}, []
-    ops = {(x, k): [] for x in range(NX) for k in (0, 1)}
-    have, ready, late = {}, {}, {}
-
-    def got(x, k, z, item, t):
-        assert (x, k, z, item) not in late
-        late[x, k, z, item] = t
-        have[x, k, item] = max(have.get((x, k, item), 0.0), t)
-        for i in need.get((x, k, item), ()):
-            heapq.heappush(heap, (t, ms[i][6], i, z))
-
+    devices = [(x, k) for x in range(NX) for k in (0, 1)]
+    need, queues, flying, have, ready, clock = {}, {}, {}, {}, {}, 0.0
     for i, m in enumerate(ms):
         need.setdefault((m[2], m[4], m[0]), []).append(i)
-    for x in range(NX):
-        for k in (0, 1):
-            for z in (0, 1):
-                for h in (0, 1):
-                    got(x, k, z, ("S", 0, x, h), 0.0)
-                    got(x, k, z, ("A", 0, h), 0.0)
-            ops[x, k].append((0.0, 9, 0, "share", 4 + k))
-    while heap:
-        t, rank, i, z = heapq.heappop(heap)
-        _, kind, xs, xd, k, item2, _ = ms[i]
-        if kind == "zz":
-            links = [("even", z, xs)]
-        elif kind in ("z+", "z-"):
-            way = 0 if kind == "z+" else 1
-            links = [("even", way, xs), ("odd", way, xs)]
-        else:
-            links = [(kind, xs, z)]
-        start = max([t] + [free.get(link, 0.0) for link in links])
-        for link in links:
-            free[link] = start + 0.5
-        ready[i] = max(ready.get(i, 0.0), t)
-        got(xd, k, 1 - z if kind == "zz" else z, item2, start + 0.5 + HOP * len(links))
+    ops = {device: [(0.0, 9, 0, "share", 4 + device[1])] for device in devices}
+    coming = [(0.0, x, k, z, item) for x, k in devices for z in (0, 1) for h in (0, 1)
+              for item in (("S", 0, x, h), ("A", 0, h))]
+    heapq.heapify(coming)
+    while coming or flying:
+        while coming and coming[0][0] <= clock + 1e-9:
+            t, x, k, z, item = heapq.heappop(coming)
+            have[x, k, item] = max(have.get((x, k, item), 0.0), t)
+            for i in need.get((x, k, item), ()):
+                kind = ("z-" if z else "z+") if ms[i][1] == "zz" else ms[i][1]
+                heapq.heappush(queues.setdefault((kind, x, k, z), []), (t, ms[i][6], i, z))
+                ready[i] = max(ready.get(i, 0.0), t)
+        for key, queue in queues.items():
+            if queue and key not in flying:
+                _, _, i, z = heapq.heappop(queue)
+                _, kind, x, *_ = ms[i]
+                if kind == "zz":
+                    links = [("even", "z-" if z else "z+", x)]
+                elif kind in ("z+", "z-"):
+                    links = [("even", kind, x), ("odd", kind, x)]
+                else:
+                    links = [(kind, x, z)]
+                flying[key] = [i, z, 0.5, links]
+        users = collections.Counter(link for flight in flying.values() for link in flight[3])
+        rate = {key: min(1.0 / users[link] for link in flight[3]) for key, flight in flying.items()}
+        step = min([flight[2] / rate[key] for key, flight in flying.items()], default=1e9)
+        if coming:
+            step = min(step, max(coming[0][0] - clock, 0.0))
+        clock += step
+        for key, flight in list(flying.items()):
+            flight[2] -= rate[key] * step
+            if flight[2] <= 1e-7:
+                i, z, _, links = flying.pop(key)
+                _, kind, _, xd, k, item, _ = ms[i]
+                heapq.heappush(coming, (clock + HOP * len(links), xd, k, 1 - z if kind == "zz" else z, item))
     for i, (item, kind, xs, xd, k, item2, rank) in enumerate(ms):
         ops[xs, k].append((ready[i], rank, i, "send", item, kind, xd, item2))
         ops[xd, k].append((have[xd, k, item2], -1, i, "wait", item2))
@@ -190,7 +195,7 @@
     return ref[0:rows, :].astype(jnp.int32).astype(F32) * (scale_of(level) * (1.0 / TOP))
 
 
-def kernel(n_wide, naux, nloc, omap, occ, x, xt, kept, vir, out, bs, gt, va, tt, work, keep, sy, ry, sn, rn,
+def kernel(n_wide, naux, nloc, rounds, omap, occ, kept, x, vir, out, bs, gt, va, tt, work, keep, sy, ry, sn, rn,
            loc_sem, w_send, w_recv, s_send, s_recv, g_recv, sy_sem, ry_sem, sn_sem, rn_sem):
     wide = lax.axis_index("wide")
     narrow = lax.axis_index("narrow")
@@ -221,8 +226,6 @@
 
     local = [
         pltpu.make_async_copy(x, bs.at[own, pl.ds(0, naux)], loc_sem.at[0]),
-        pltpu.make_async_copy(kept, bs.at[own, pl.ds(naux, EXTRA)], loc_sem.at[1]),
-        pltpu.make_async_copy(xt, gt.at[0], loc_sem.at[2]),
     ]
     for c in local:
         c.start()
@@ -230,9 +233,16 @@
     greeted = [sib, *to.values()]
     for device in greeted:
         pl.semaphore_signal(barrier, inc=1, device_id=device, device_id_type=MESH)
-    pl.semaphore_wait(barrier, len(greeted))
+    rows16 = lax.broadcasted_iota(jnp.int32, (EXTRA, nloc), 0)
+    weights = jnp.zeros((EXTRA, nloc), F32)
+    for r in range(rounds):
+        weights = jnp.where(rows16 == r, kept[r].astype(F32), weights)
+    bs[own, naux : naux + EXTRA, :] = weights.astype(BF16)
     for c in local:
         c.wait()
+    for r in range(0, naux, nloc):
+        gt[0, :, r : r + nloc] = bs[own, r : r + nloc, :].T
+    pl.semaphore_wait(barrier, len(greeted))
 
     def remote(src, dst, s_sem, r_sem, device):
         return pltpu.make_async_remote_copy(src_ref=src, dst_ref=dst, send_sem=s_sem, recv_sem=r_sem,
@@ -288,7 +298,6 @@
         va[g] = jnp.broadcast_to(row, (nloc, nloc)).T
     vb = vir[pl.ds(narrow, 1), :]
     e_own = occ[omap[wide]]
-    rows16 = lax.broadcasted_iota(jnp.int32, (EXTRA, nloc), 0)
 
     def block(q, g0, ng):
         pair = jnp.concatenate([bs[2 * q, 0:naux, :], bs[2 * q + 1, 0:naux, :]], axis=1)
@@ -333,10 +342,6 @@
     blocks(0, 5, 5, 2)
     run(5)
     blocks(5, 6, 0, 7, True)
-    run(6)
-    run(7)
-    blocks(0, 6, 7, 1)
-
     quarter = naux // 4
 
     def rows_of(part):
@@ -392,12 +397,15 @@
             encode(value, sn.at[8 + 2 * stage + way])
             n_copy(8 + 2 * stage + way, beside(way)).start()
 
+    y_step(1)
+    z_step(1)
+    run(6)
+    run(7)
+    blocks(0, 6, 7, 1)
     y_step(0)
     z_step(3)
-    y_step(1)
-    z_step(1)
+    z_step(2)
     y_step(2)
-    z_step(2)
     n_step(0)
     z_step(0)
     n_step(1)
@@ -436,8 +444,7 @@
     n_wide = lax.axis_size("wide")
     n_narrow = lax.axis_size("narrow")
     x = three_index.reshape(naux, nloc)
-    kept = jnp.pad(pair_kept, ((0, EXTRA - pair_kept.shape[0]), (0, 0))).astype(BF16)
-    kept = jnp.broadcast_to(kept, (EXTRA, nloc))
+    kept = pair_kept.reshape(-1)
     vir = vir_energy.reshape(n_narrow, nloc)
     quarter = naux // 4
     vmem = functools.partial(pl.BlockSpec, memory_space=pltpu.VMEM)
@@ -445,9 +452,9 @@
     hbm = functools.partial(pl.BlockSpec, memory_space=pl.ANY)
     dma = pltpu.SemaphoreType.DMA
     density = pl.pallas_call(
-        functools.partial(kernel, n_wide, naux, nloc),
+        functools.partial(kernel, n_wide, naux, nloc, kept.shape[0]),
         out_shape=jax.ShapeDtypeStruct((naux, nloc), F32),
-        in_specs=[smem(), smem(), hbm(), hbm(), hbm(), vmem()],
+        in_specs=[smem(), smem(), smem(), hbm(), vmem()],
         out_specs=vmem(),
         scratch_shapes=[
             pltpu.VMEM((SLOTS + RELAYS, naux + EXTRA, nloc), BF16),
@@ -460,7 +467,7 @@
             pltpu.VMEM((6, quarter + EXTRA, 2 * nloc), jnp.int16),
             pltpu.VMEM((16, quarter + EXTRA, nloc), jnp.int16),
             pltpu.VMEM((16, quarter + EXTRA, nloc), jnp.int16),
-            dma((3,)),
+            dma((1,)),
             dma((32,)),
             dma((SLOTS + RELAYS, 2)),
             dma((6,)),
@@ -474,7 +481,7 @@
         compiler_params=pltpu.CompilerParams(
             collective_id=0, has_side_effects=True, vmem_limit_bytes=60 * 1024 * 1024
         ),
-    )(orbital_map, occ_energy, x, x.T, kept, vir)
+    )(orbital_map, occ_energy, kept, x, vir)
     return density.reshape(1, naux, nloc)
 
 

time: 136 us -> 124 us (0.912)
  the two profiles are of different devices: /device:TPU:7 before, /device:TPU:3 now
where the time goes in v3:
time: 124 us
  Pallas kernels  121 us (98%)
  local copies, waits for them, and re-layouts  2.65 us (2%)
    pallas_call x1, Pallas kernels, per_device(): pl.pallas_call(functools.partial(kernel, n_wide, naux, nloc, kept.shape[0...  121 us
    unnamed x1, local copies, waits for them, and re-layouts  2.65 us

profile of v3, /device:TPU:3, one launch (start us, length us, event | category | flops | bytes accessed | tf_op | source)
XLA Modules:
  0.0 124.1 jit_solution(13393838121294982027)
XLA Ops:
  0.0 121.5 %shard_map.55 = f32[3072,128]{1,0:T(8,128)} custom-call(s32[32]{0:T(128)} %omap.1, f32[32]{0:T(128)} %occ.1, s32[6]{0:T(128)} %bitcast.7, bf16[3072,128]{1,0:T(8,128)(2,1)} %bitcast.5, f32[8,128]{1,0:T(8,128)} %bitcast.6), custom_call_target="tpu_custom_call" | custom-call | tf_op jit(solution)/shard_map/pallas_call | solution.py:454
  121.5 2.7 %copy.7 = f32[1,3072,128]{2,1,0:T(8,128)} copy(f32[1,3072,128]{2,1,0:T(8,128)} %bitcast.4) | data formatting | bytes 3145728

commit v4 on v3

--- a/solution.py
+++ b/solution.py
@@ -15,6 +15,7 @@
 
 NX, NY, NZL = 4, 4, 2
 EXTRA = 16
+Y_ROWS = 832
 SLOTS = 12
 LN2 = 0.6931471805599453
 FINE = 64.0
@@ -80,7 +81,7 @@
                 out.append((("A", g0, h), kind, x, x, k, ("A", g1, h), rank))
 
             for h in (0, 1):
-                ag(0, "zz", 4, h, 1 + 0.1 * h)
+                ag(0, "zz", 4, h, 3 + 0.1 * h)
                 ag(0, "y+", 2, h, 2 + 0.1 * h)
                 ag(0, "y-", 1, 1 - h, 2 + 0.1 * h)
                 ag(4, "y+", 6, h, 3)
@@ -342,15 +343,19 @@
     blocks(0, 5, 5, 2)
     run(5)
     blocks(5, 6, 0, 7, True)
-    quarter = naux // 4
-
-    def rows_of(part):
-        return pl.ds(pl.multiple_of(part * quarter, quarter), quarter)
-
-    def tile(p, part):
-        lhs = jnp.concatenate([bs[s, rows_of(part), :] for s in range(SLOTS)], axis=1)
+    y_rows = Y_ROWS
+    z_rows = naux // 2 - y_rows
+
+    def y_part(part):
+        return pl.ds(pl.multiple_of(part * y_rows, 32), y_rows)
+
+    def z_part(part):
+        return pl.ds(pl.multiple_of(2 * y_rows + part * z_rows, 32), z_rows)
+
+    def tile(p, rows):
+        lhs = jnp.concatenate([bs[s, rows, :] for s in range(SLOTS)], axis=1)
         cols = pl.ds(pl.multiple_of(p * 2 * nloc, 2 * nloc), 2 * nloc)
-        work[0:quarter, :] = jnp.dot(lhs, tt[:, cols], preferred_element_type=F32)
+        work[0 : rows.size, :] = jnp.dot(lhs, tt[:, cols], preferred_element_type=F32)
 
     def beside(way):
         return (wide, jnp.where(way == 0, right[1], left[1]))
@@ -358,22 +363,24 @@
     def y_copy(i, way):
         return remote(sy.at[i], ry.at[i], sy_sem.at[i], ry_sem.at[i], beside(way))
 
-    def n_copy(i, device):
-        return remote(sn.at[i], rn.at[i], sn_sem.at[i], rn_sem.at[i], device)
+    def n_copy(i, device, rows):
+        part = pl.ds(0, rows + EXTRA)
+        return remote(sn.at[i, part], rn.at[i, part], sn_sem.at[i], rn_sem.at[i], device)
 
     def took_y(i):
         arrived(ry.at[i], ry_sem.at[i])
-        return decode(ry.at[i], quarter)
-
-    def took_n(i):
-        arrived(rn.at[i], rn_sem.at[i])
-        return decode(rn.at[i], quarter)
+        return decode(ry.at[i], y_rows)
+
+    def took_n(i, rows):
+        part = rn.at[i, pl.ds(0, rows + EXTRA)]
+        arrived(part, rn_sem.at[i])
+        return decode(part, rows)
 
     def y_step(stage):
         @pl.loop(0, 2)
         def _(way):
-            tile(3 if stage == 0 else 1 + way, 1 - way if stage == 1 else way)
-            value = work[0:quarter, :]
+            tile(3 if stage == 0 else 1 + way, y_part(1 - way if stage == 1 else way))
+            value = work[0:y_rows, :]
             if stage == 2:
                 value = value + took_y(way)
             encode(value, sy.at[2 * stage + way])
@@ -382,20 +389,20 @@
     def z_step(p):
         @pl.loop(0, 2)
         def _(j):
-            tile(p, 2 + j)
-            keep[2 * p + j] = work[0:quarter, 0:nloc]
-            encode(work[0:quarter, nloc : 2 * nloc], sn.at[2 * p + j])
-            n_copy(2 * p + j, zpart).start()
+            tile(p, z_part(j))
+            keep[2 * p + j] = work[0:z_rows, 0:nloc]
+            encode(work[0:z_rows, nloc : 2 * nloc], sn.at[2 * p + j])
+            n_copy(2 * p + j, zpart, z_rows).start()
 
     def n_step(stage):
         @pl.loop(0, 2)
         def _(way):
             i = 6 + way if stage == 0 else 2 * (1 + way) + (1 - way if stage == 1 else way)
-            value = keep[i] + took_n(i)
+            value = keep[i] + took_n(i, z_rows)
             if stage == 2:
-                value = value + took_n(8 + way)
+                value = value + took_n(8 + way, z_rows)
             encode(value, sn.at[8 + 2 * stage + way])
-            n_copy(8 + 2 * stage + way, beside(way)).start()
+            n_copy(8 + 2 * stage + way, beside(way), z_rows).start()
 
     y_step(1)
     z_step(1)
@@ -412,21 +419,21 @@
 
     @pl.loop(0, 2)
     def _(part):
-        tile(0, part)
-        total = work[0:quarter, :] + took_y(4 - 2 * part) + took_y(3 + 2 * part)
-        out[rows_of(part), :] = total[:, 0:nloc]
+        tile(0, y_part(part))
+        total = work[0:y_rows, :] + took_y(4 - 2 * part) + took_y(3 + 2 * part)
+        out[y_part(part), :] = total[:, 0:nloc]
         encode(total[:, nloc : 2 * nloc], sn.at[14 + part])
-        n_copy(14 + part, zpart).start()
+        n_copy(14 + part, zpart, y_rows).start()
 
     n_step(2)
 
     @pl.loop(0, 2)
     def _(j):
-        out[rows_of(2 + j), :] = keep[j] + took_n(j) + took_n(12 - 2 * j) + took_n(11 + 2 * j)
+        out[z_part(j), :] = keep[j] + took_n(j, z_rows) + took_n(12 - 2 * j, z_rows) + took_n(11 + 2 * j, z_rows)
 
     @pl.loop(0, 2)
     def _(part):
-        out[rows_of(part), :] += took_n(14 + part)
+        out[y_part(part), :] += took_n(14 + part, y_rows)
 
     run(0, True)
 
@@ -434,9 +441,13 @@
     def _(i):
         y_copy(i, i % 2).wait_send()
 
-    @pl.loop(0, 16)
+    @pl.loop(0, 14)
     def _(i):
-        n_copy(i, sib).wait_send()
+        n_copy(i, sib, z_rows).wait_send()
+
+    @pl.loop(14, 16)
+    def _(i):
+        n_copy(i, sib, y_rows).wait_send()
 
 
 def per_device(three_index, orbital_map, occ_energy, vir_energy, pair_kept):
@@ -446,7 +457,6 @@
     x = three_index.reshape(naux, nloc)
     kept = pair_kept.reshape(-1)
     vir = vir_energy.reshape(n_narrow, nloc)
-    quarter = naux // 4
     vmem = functools.partial(pl.BlockSpec, memory_space=pltpu.VMEM)
     smem = functools.partial(pl.BlockSpec, memory_space=pltpu.SMEM)
     hbm = functools.partial(pl.BlockSpec, memory_space=pl.ANY)
@@ -462,11 +472,11 @@
             pltpu.VMEM((8, nloc, nloc), F32),
             pltpu.VMEM((SLOTS * nloc, 8 * nloc), BF16),
             pltpu.VMEM((8 * nloc, 2 * nloc), F32),
-            pltpu.VMEM((8, quarter, nloc), F32),
-            pltpu.VMEM((6, quarter + EXTRA, 2 * nloc), jnp.int16),
-            pltpu.VMEM((6, quarter + EXTRA, 2 * nloc), jnp.int16),
-            pltpu.VMEM((16, quarter + EXTRA, nloc), jnp.int16),
-            pltpu.VMEM((16, quarter + EXTRA, nloc), jnp.int16),
+            pltpu.VMEM((8, naux // 2 - Y_ROWS, nloc), F32),
+            pltpu.VMEM((6, Y_ROWS + EXTRA, 2 * nloc), jnp.int16),
+            pltpu.VMEM((6, Y_ROWS + EXTRA, 2 * nloc), jnp.int16),
+            pltpu.VMEM((16, Y_ROWS + EXTRA, nloc), jnp.int16),
+            pltpu.VMEM((16, Y_ROWS + EXTRA, nloc), jnp.int16),
             dma((1,)),
             dma((32,)),
             dma((SLOTS + RELAYS, 2)),

time: 124 us -> 119 us (0.960)
  the two profiles are of different devices: /device:TPU:3 before, /device:TPU:7 now
where the time goes in v4:
time: 119 us; the launch traced here: 117 us
  Pallas kernels  114 us (96%)
  local copies, waits for them, and re-layouts  2.65 us (2%)
    pallas_call x1, Pallas kernels, per_device(): pl.pallas_call(functools.partial(kernel, n_wide, naux, nloc, kept.shape[0...  114 us
    unnamed x1, local copies, waits for them, and re-layouts  2.65 us

profile of v4, /device:TPU:7, one launch (start us, length us, event | category | flops | bytes accessed | tf_op | source)
XLA Modules:
  0.0 117.1 jit_solution(8949964145019203557)
XLA Ops:
  0.0 114.5 %shard_map.55 = f32[3072,128]{1,0:T(8,128)} custom-call(s32[32]{0:T(128)} %omap.1, f32[32]{0:T(128)} %occ.1, s32[6]{0:T(128)} %bitcast.7, bf16[3072,128]{1,0:T(8,128)(2,1)} %bitcast.5, f32[8,128]{1,0:T(8,128)} %bitcast.6), custom_call_target="tpu_custom_call" | custom-call | tf_op jit(solution)/shard_map/pallas_call | solution.py:464
  114.5 2.7 %copy.7 = f32[1,3072,128]{2,1,0:T(8,128)} copy(f32[1,3072,128]{2,1,0:T(8,128)} %bitcast.4) | data formatting | bytes 3145728

commit v5 on v4

--- a/solution.py
+++ b/solution.py
@@ -24,11 +24,11 @@
 
 HOP = 0.2
 ROUTES = {
-    (3, 1): ((3, ((3, 0), (0, 1), (3, 2))),),
+    (3, 1): ((3, ((3, 0), (0, 1), (3, 2))), (3, ((3, 0), (3, 2), (2, 1)))),
     (3, 0): ((0, ((0, 1),)),),
     (2, 1): ((1, ((1, 0),)),),
     (2, 0): ((2, ((2, 1), (1, 0))),),
-    (1, 1): ((1, ((1, 0),)), (0, ())),
+    (1, 1): ((0, ()), (1, ((1, 0),))),
 }
 ORDER = ((2, 3, 4, 5, 1, 0), (1, 2, 3, 4, 5, 0), (1, 2, 3, 0, 5, 4), (0, 1, 2, 5, 3, 4))
 PHASES = ((3, 3), (4, 5), (5, 5), (5, 7), (6, 7), (6, 8))
@@ -412,9 +412,9 @@
     y_step(0)
     z_step(3)
     z_step(2)
+    z_step(0)
     y_step(2)
     n_step(0)
-    z_step(0)
     n_step(1)
 
     @pl.loop(0, 2)

time: 119 us -> 119 us (level)
  no operation moved by 1% of the time
where the time goes in v5:
time: 119 us; the launch traced here: 117 us
  Pallas kernels  115 us (97%)
  local copies, waits for them, and re-layouts  2.65 us (2%)
    pallas_call x1, Pallas kernels, per_device(): pl.pallas_call(functools.partial(kernel, n_wide, naux, nloc, kept.shape[0...  115 us
    unnamed x1, local copies, waits for them, and re-layouts  2.65 us

profile of v5, /device:TPU:7, one launch (start us, length us, event | category | flops | bytes accessed | tf_op | source)
XLA Modules:
  0.0 117.2 jit_solution(17039254047329721277)
XLA Ops:
  0.0 114.5 %shard_map.55 = f32[3072,128]{1,0:T(8,128)} custom-call(s32[32]{0:T(128)} %omap.1, f32[32]{0:T(128)} %occ.1, s32[6]{0:T(128)} %bitcast.7, bf16[3072,128]{1,0:T(8,128)(2,1)} %bitcast.5, f32[8,128]{1,0:T(8,128)} %bitcast.6), custom_call_target="tpu_custom_call" | custom-call | tf_op jit(solution)/shard_map/pallas_call | solution.py:464
  114.5 2.7 %copy.7 = f32[1,3072,128]{2,1,0:T(8,128)} copy(f32[1,3072,128]{2,1,0:T(8,128)} %bitcast.4) | data formatting | bytes 3145728
